TPU v7x, 32 devices: a whole 2x2x4 slice. The times are simulated.
32 devices in a mesh: wide: 8 (over z, x), narrow: 4 (over y, core).
Axes of the slice: x: 2, y: 2, z: 4, core: 2. Of those that a mesh axis runs over, the one named last changes fastest.
Arguments:
- points: bfloat16 [32768, 256], P('wide'), may hold values from -6 to 6
- q_init: float32 [16, 32768], P(None, 'wide'), may hold values from -80 to 80
- pairs: int32 [2, 2048], P(None, ('wide', 'narrow')), may hold values from 0 to 255, as said below
Outputs:
- basis: float32 [16, 32768], P(None, 'wide')
- coeffs: float32 [3, 2, 16, 16], replicated
Inputs may be any that keep to these rules, and one draw needn't show every extreme that they name: `pairs`: pair number g * 4 * 64 + m * 64 + o * 8 + c (g < 8, m < 4, o < 8, c < 8) has its first block in g * 32 .. (g + 1) * 32 - 1 and its second block in o * 32 .. (o + 1) * 32 - 1; the two ends of a pair differ.
All inputs are finite; a program needn't handle non-finite values.
Results may differ from a plain program's by a relative error of at most 0.0015.
Values may be sent and summed in bfloat16 or wider, within the bound.
A program may use at most 64 MiB of HBM per device.

v0:
```python
import jax
import jax.numpy as jnp
from jax import lax
from jax.sharding import PartitionSpec as P

BS = 128
STEPS = 3
KERNEL_FACTOR = 3.0
EPSILON = 1e-06
HIGH = lax.Precision.HIGHEST
pair_group = 32


def unit_rows(points):
    wide32 = points.astype(jnp.float32)
    scaled = wide32 * lax.rsqrt(jnp.sum(wide32 * wide32, axis=-1, keepdims=True) + EPSILON)
    return scaled.astype(jnp.bfloat16)


def tile_terms(first_pts, second_pts, first_vec, second_vec):
    inner_products = jnp.einsum(
        "paf,pbf->pab", first_pts, second_pts, preferred_element_type=jnp.float32
    )
    kernel_values = jnp.exp(KERNEL_FACTOR * (inner_products - 1.0))
    to_first = jnp.einsum("pab,prb->pra", kernel_values, second_vec, precision=HIGH)
    to_second = jnp.einsum("pab,pra->prb", kernel_values, first_vec, precision=HIGH)
    return (to_first, to_second)


def per_device(points, q_init, pairs):
    wide_count = lax.axis_size("wide")
    wide_pos = lax.axis_index("wide")
    own_blocks = points.shape[0] // BS
    width = points.shape[1]
    vec_rows = q_init.shape[0]
    pair_count = pairs.shape[1]
    capacity = pair_count // wide_count
    total_points = own_blocks * BS * wide_count
    unit = unit_rows(points).reshape(own_blocks, BS, width)
    first_local = pairs[0] - wide_pos * own_blocks
    wanted = pairs[1].reshape(wide_count, capacity)
    local_ids = (
        lax.all_to_all(wanted, "wide", split_axis=0, concat_axis=0, tiled=True)
        - wide_pos * own_blocks
    )
    replies = lax.all_to_all(unit[local_ids], "wide", split_axis=0, concat_axis=0, tiled=True)
    second_pts = replies
    second_pts = second_pts.reshape(pair_count, BS, width)
    targets = jnp.concatenate([first_local, local_ids.reshape(pair_count)], axis=0)
    owners = (jnp.arange(own_blocks, dtype=jnp.int32)[:, None] == targets[None, :]).astype(
        jnp.float32
    )

    def grouped(values):
        return values.reshape((pair_count // pair_group, pair_group) + values.shape[1:])

    def single_group(items):
        first_ids, second_p, first_v, second_v = items
        return tile_terms(unit[first_ids], second_p, first_v, second_v)

    def gram_sums(values):
        return lax.psum(values, "wide")

    gram0 = gram_sums(jnp.dot(q_init, q_init.T, precision=HIGH)) / total_points
    factor0 = jnp.linalg.cholesky(gram0)
    present_portion = lax.linalg.triangular_solve(factor0, q_init, left_side=True, lower=True)
    current = present_portion
    previous = jnp.zeros_like(present_portion)
    last = jnp.zeros((vec_rows, vec_rows), jnp.float32)
    records = []
    for step in range(STEPS):
        rows = current.reshape(vec_rows, own_blocks, BS).transpose(1, 0, 2)
        second_vec = lax.all_to_all(
            rows[local_ids], "wide", split_axis=0, concat_axis=0, tiled=True
        ).reshape(pair_count, vec_rows, BS)
        first_vec = rows[first_local]
        to_first, to_second = lax.map(
            single_group,
            (grouped(first_local), grouped(second_pts), grouped(first_vec), grouped(second_vec)),
        )
        to_first = to_first.reshape(pair_count, vec_rows * BS)
        returned = lax.all_to_all(
            to_second.reshape(wide_count, capacity, vec_rows * BS),
            "wide",
            split_axis=0,
            concat_axis=0,
            tiled=True,
        )
        terms = jnp.concatenate([to_first, returned.reshape(pair_count, vec_rows * BS)], axis=0)
        summed_blocks = jnp.dot(owners, terms, precision=HIGH)
        summed_blocks = lax.psum(summed_blocks, "narrow")
        image = summed_blocks.reshape(-1, vec_rows, BS).transpose(1, 0, 2).reshape(vec_rows, -1)
        residual = image - jnp.dot(last.T, previous, precision=HIGH)
        raw, cross, basis_gram = gram_sums(
            (
                jnp.dot(residual, residual.T, precision=HIGH),
                jnp.dot(present_portion, residual.T, precision=HIGH),
                jnp.dot(present_portion, present_portion.T, precision=HIGH),
            )
        )
        along = cross / total_points
        raw = raw / total_points
        basis_gram = basis_gram / total_points
        remainder = residual - jnp.dot(along.T, present_portion, precision=HIGH)
        squared = jnp.dot(along.T, along, precision=HIGH)
        gram = (
            raw
            - 2.0 * squared
            + jnp.dot(along.T, jnp.dot(basis_gram, along, precision=HIGH), precision=HIGH)
        )
        factor = jnp.linalg.cholesky(gram)
        records.append(jnp.stack([along, factor]))
        previous = present_portion
        last = factor
        present_portion = lax.linalg.triangular_solve(factor, remainder, left_side=True, lower=True)
        current = present_portion
    return (current, jnp.stack(records))


def solution(mesh):
    placed = (P("wide", None), P(None, "wide"), P(None, ("wide", "narrow")))
    return jax.shard_map(
        per_device, mesh=mesh, in_specs=placed, out_specs=(P(None, "wide"), P()), check_vma=False
    )
```

profile of v0, /device:TPU:0, one launch (start us, length us, event | category | flops | bytes accessed | tf_op | source)
XLA Modules:
  0.0 559.8 jit_solution(13503507722654973966)
XLA Ops:
  8.6 7.3 %all-to-all-start = ((s32[8,1,8]{2,1,0:T(1,128)}), s32[8,1,8]{2,1,0:T(1,128)S(1)}, u32[]{:S(2)}, u32[]{:S(2)}) async-start(s32[8,1,8]{2,1,0:T(1,128)} %bitcast.22), calls=%async_computation | async-start | bytes 8192 | tf_op jit(solution)/shard_map/all_to_all | solution.py:43
  16.4 22.1 %psum.91 = f32[16,16]{1,0:T(8,128)S(1)} all-reduce(f32[16,16]{1,0:T(8,128)S(1)} %fusion.187), channel_id=1, replica_groups=mesh['wide'=8,'narrow'=4] {'wide'}, use_global_device_ids=true, to_apply=%region_1.0 | all-reduce | flops 256 | bytes 2048 | tf_op jit(solution)/shard_map/psum | solution.py:62
  43.1 2.2 fusion.78
  46.9 3.5 all-to-all-start.1
  50.4 1.9 fusion.79
  52.3 2.8 gather_fusion.4
  55.1 5.6 %all-to-all-done.1 = f32[8,8,16,128]{3,2,1,0:T(8,128)S(1)} async-done(((f32[8,8,16,128]{3,2,1,0:T(8,128)}), f32[8,8,16,128]{3,2,1,0:T(8,128)S(1)}, u32[]{:S(2)}, u32[]{:S(2)}) %all-to-all-start.1) | async-done | bytes 524320 | tf_op jit(solution)/shard_map/all_to_all | solution.py:73
  60.7 4.7 all-to-all-start.2
  65.5 1.5 gather_fusion.5
  67.0 87.2 %all-to-all-done.2 = bf16[8,8,128,256]{3,2,1,0:T(8,128)(2,1)} async-done(((bf16[8,8,128,256]{3,2,1,0:T(8,128)(2,1)}), bf16[8,8,128,256]{3,2,1,0:T(8,128)(2,1)}, u32[]{:S(2)}, u32[]{:S(2)}) %all-to-all-start.2) | async-done | bytes 4194336 | tf_op jit(solution)/shard_map/all_to_all | solution.py:46
  155.9 23.6 %while.42 = (s32[]{:T(128)}, f32[2,32,16,128]{3,2,1,0:T(8,128)}, f32[2,32,16,128]{3,2,1,0:T(8,128)}, f32[2,32,16,128]{3,2,1,0:T(8,128)S(1)}, s32[2,32]{1,0:T(2,1...) while((s32[]{:T(128)}, f32[2,32,16,128]{3,2,1,0:T(8,128)}, ...), condition=%wide.region_5.8_spmd, body=%wide.region_4.7_spmd.sunk | while | flops 471860320 | bytes 17833084 | solution.py:77
  155.9 2.0 gather_fusion
  158.0 2.9 fusion.264
  160.9 4.1 fusion.265
  165.0 2.8 fusion.266
  167.7 2.0 gather_fusion
  169.8 2.9 fusion.264
  172.7 4.1 fusion.265
  176.8 2.8 fusion.266
  179.5 1.9 reshape.254
  181.5 3.5 all-to-all-start.3
  185.2 2.0 copy.75
  187.2 12.4 %all-to-all-done.3 = f32[8,8,2048]{2,1,0:T(8,128)S(1)} async-done(((f32[8,8,2048]{2,1,0:T(8,128)}), f32[8,8,2048]{2,1,0:T(8,128)S(1)}, u32[]{:S(2)}, u32[]{:S(2)}) %all-to-all-start.3) | async-done | bytes 524320 | tf_op jit(solution)/shard_map/all_to_all | solution.py:82
  199.6 1.5 convolution_bitcast_fusion.2
  202.4 31.1 %all-reduce.7.cloned.1.call-done = f32[16,4096]{1,0:T(8,128)} async-done(((f32[16,4096]{1,0:T(8,128)}), f32[16,4096]{1,0:T(8,128)}) %all-reduce.7.cloned.1.call-update) | async-done | bytes 262160 | tf_op jit(solution)/shard_map/psum | solution.py:91
  235.6 37.1 %all-reduce.2 = (f32[16,16]{1,0:T(8,128)S(1)}, f32[16,16]{1,0:T(8,128)S(1)}, f32[16,16]{1,0:T(8,128)S(1)}) all-reduce(f32[16,16]{1,0:T(8,128)S(1)} %fusion.189, f32[16,16]{1,0:T(8,128)S(1)} %fusion.188, f32[16,16]{1,0:T(8,128)S(1)} %fusion.190), channel_id=1, replica_groups=mesh['wide'=8,'narrow'=4] {'wide'}, use_global_device_ids=true, to_apply=%region_8.11 | all-reduce | flops 768 | bytes 6144 | tf_op jit(solution)/shard_map/psum | solution.py:62
  273.8 1.5 cholesky.85
  279.7 4.1 all-to-all-start.4
  285.3 8.8 %all-to-all-done.4 = f32[8,8,16,128]{3,2,1,0:T(8,128)} async-done(((f32[8,8,16,128]{3,2,1,0:T(8,128)}), f32[8,8,16,128]{3,2,1,0:T(8,128)}, u32[]{:S(2)}, u32[]{:S(2)}) %all-to-all-start.4) | async-done | bytes 524320 | tf_op jit(solution)/shard_map/all_to_all | solution.py:73
  295.8 25.6 %while.43 = (s32[]{:T(128)}, f32[2,32,16,128]{3,2,1,0:T(8,128)}, f32[2,32,16,128]{3,2,1,0:T(8,128)}, f32[2,32,16,128]{3,2,1,0:T(8,128)}, s32[2,32]{1,0:T(2,128)S...) while((s32[]{:T(128)}, f32[2,32,16,128]{3,2,1,0:T(8,128)}, ...), condition=%wide.region_11.14_spmd, body=%wide.region_10.13_spmd.sunk | while | flops 471860320 | bytes 17833084 | solution.py:77
  295.8 2.0 gather_fusion.1
  297.8 2.9 fusion.272
  300.7 5.1 fusion.273
  305.8 2.7 fusion.274
  308.6 2.0 gather_fusion.1
  310.6 2.9 fusion.272
  313.5 5.1 fusion.273
  318.6 2.8 fusion.274
  321.3 1.9 reshape.261
  323.2 3.7 all-to-all-start.5
  326.9 2.0 copy.74
  329.0 8.2 %all-to-all-done.5 = f32[8,8,2048]{2,1,0:T(8,128)S(1)} async-done(((f32[8,8,2048]{2,1,0:T(8,128)}), f32[8,8,2048]{2,1,0:T(8,128)S(1)}, u32[]{:S(2)}, u32[]{:S(2)}) %all-to-all-start.5) | async-done | bytes 524320 | tf_op jit(solution)/shard_map/all_to_all | solution.py:82
  337.2 1.5 convolution_bitcast_fusion.1
  339.9 30.2 %all-reduce.9.cloned.1.call-done = f32[16,4096]{1,0:T(8,128)} async-done(((f32[16,4096]{1,0:T(8,128)}), f32[16,4096]{1,0:T(8,128)}) %all-reduce.9.cloned.1.call-update) | async-done | bytes 262160 | tf_op jit(solution)/shard_map/psum | solution.py:91
  370.1 1.9 convolution_subtract_fusion.3
  373.0 37.1 %all-reduce.1 = (f32[16,16]{1,0:T(8,128)S(1)}, f32[16,16]{1,0:T(8,128)S(1)}, f32[16,16]{1,0:T(8,128)S(1)}) all-reduce(f32[16,16]{1,0:T(8,128)S(1)} %fusion.192, f32[16,16]{1,0:T(8,128)S(1)} %fusion.191, f32[16,16]{1,0:T(8,128)S(1)} %fusion.193), channel_id=1, replica_groups=mesh['wide'=8,'narrow'=4] {'wide'}, use_global_device_ids=true, to_apply=%region_14.17 | all-reduce | flops 768 | bytes 6144 | tf_op jit(solution)/shard_map/psum | solution.py:62
  411.2 1.5 cholesky.96
  417.0 4.4 all-to-all-start.6
  422.8 8.6 %all-to-all-done.6 = f32[8,8,16,128]{3,2,1,0:T(8,128)} async-done(((f32[8,8,16,128]{3,2,1,0:T(8,128)}), f32[8,8,16,128]{3,2,1,0:T(8,128)}, u32[]{:S(2)}, u32[]{:S(2)}) %all-to-all-start.6) | async-done | bytes 524320 | tf_op jit(solution)/shard_map/all_to_all | solution.py:73
  433.1 25.6 %while.44 = (s32[]{:T(128)}, f32[2,32,16,128]{3,2,1,0:T(8,128)}, f32[2,32,16,128]{3,2,1,0:T(8,128)}, f32[2,32,16,128]{3,2,1,0:T(8,128)}, s32[2,32]{1,0:T(2,128)S...) while((s32[]{:T(128)}, f32[2,32,16,128]{3,2,1,0:T(8,128)}, ...), condition=%wide.region_17.20_spmd, body=%wide.region_16.19_spmd.sunk | while | flops 471860320 | bytes 17833084 | solution.py:77
  433.1 2.0 gather_fusion.2
  435.1 2.9 fusion.280
  438.0 5.1 fusion.281
  443.1 2.7 fusion.282
  445.9 2.0 gather_fusion.2
  447.9 2.9 fusion.280
  450.8 5.1 fusion.281
  455.9 2.8 fusion.282
  458.6 1.9 reshape.268
  460.6 3.7 all-to-all-start.7
  466.0 8.5 %all-to-all-done.7 = f32[8,8,2048]{2,1,0:T(8,128)S(1)} async-done(((f32[8,8,2048]{2,1,0:T(8,128)}), f32[8,8,2048]{2,1,0:T(8,128)S(1)}, u32[]{:S(2)}, u32[]{:S(2)}) %all-to-all-start.7) | async-done | bytes 524320 | tf_op jit(solution)/shard_map/all_to_all | solution.py:82
  475.8 30.6 %all-reduce.11.cloned.1.call-done = f32[16,4096]{1,0:T(8,128)} async-done(((f32[16,4096]{1,0:T(8,128)}), f32[16,4096]{1,0:T(8,128)}) %all-reduce.11.cloned.1.call-update) | async-done | bytes 262160 | tf_op jit(solution)/shard_map/psum | solution.py:91
  506.4 1.9 convolution_subtract_fusion.1
  509.3 37.1 %all-reduce = (f32[16,16]{1,0:T(8,128)S(1)}, f32[16,16]{1,0:T(8,128)S(1)}, f32[16,16]{1,0:T(8,128)S(1)}) all-reduce(f32[16,16]{1,0:T(8,128)S(1)} %fusion.195, f32[16,16]{1,0:T(8,128)S(1)} %fusion.194, f32[16,16]{1,0:T(8,128)S(1)} %fusion.196), channel_id=1, replica_groups=mesh['wide'=8,'narrow'=4] {'wide'}, use_global_device_ids=true, to_apply=%region_20.23 | all-reduce | flops 768 | bytes 6144 | tf_op jit(solution)/shard_map/psum | solution.py:62
  (131 shorter events, 43.6 us)
Async XLA Ops:
  7.2 8.8 %copy-start = (f32[16,4096]{1,0:T(8,128)S(1)}, f32[16,4096]{1,0:T(8,128)}, u32[]{:S(2)}) copy-start(f32[16,4096]{1,0:T(8,128)} %param.13) | copy-start | bytes 786436
  8.6 36.7 %all-to-all-start = ((s32[8,1,8]{2,1,0:T(1,128)}), s32[8,1,8]{2,1,0:T(1,128)S(1)}, u32[]{:S(2)}, u32[]{:S(2)}) async-start(s32[8,1,8]{2,1,0:T(1,128)} %bitcast.22), calls=%async_computation | async-start | bytes 8192 | tf_op jit(solution)/shard_map/all_to_all | solution.py:43
  46.9 13.9 %all-to-all-start.1 = ((f32[8,8,16,128]{3,2,1,0:T(8,128)}), f32[8,8,16,128]{3,2,1,0:T(8,128)S(1)}, u32[]{:S(2)}, u32[]{:S(2)}) async-start(f32[8,8,16,128]{3,2,1,0:T(8,128)} %bitcast.29), calls=%async_computation.1 | async-start | bytes 1048576 | tf_op jit(solution)/shard_map/all_to_all | solution.py:73
  60.7 4.7 copy-start.4
  60.7 93.5 %all-to-all-start.2 = ((bf16[8,8,128,256]{3,2,1,0:T(8,128)(2,1)}), bf16[8,8,128,256]{3,2,1,0:T(8,128)(2,1)}, u32[]{:S(2)}, u32[]{:S(2)}) async-start(bf16[8,8,128,256]{3,2,1,0:T(8,128)(2,1)} %bitcast.312), calls=%async_computation.2 | async-start | bytes 8388608 | tf_op jit(solution)/shard_map/all_to_all | solution.py:46
  160.9 4.1 copy-start.2
  172.7 4.1 copy-start.2
  181.5 18.2 %all-to-all-start.3 = ((f32[8,8,2048]{2,1,0:T(8,128)}), f32[8,8,2048]{2,1,0:T(8,128)S(1)}, u32[]{:S(2)}, u32[]{:S(2)}) async-start(f32[8,8,2048]{2,1,0:T(8,128)} %reshape.254), calls=%async_computation.3 | async-start | bytes 1048576 | tf_op jit(solution)/shard_map/all_to_all | solution.py:82
  185.0 48.6 %all-reduce.7.cloned.1.call-start = ((), (), s32[]{:S(2)}) async-start(), calls=%async_computation.8 | async-start | bytes 524288 | tf_op jit(solution)/shard_map/psum | solution.py:91
  279.7 14.4 %all-to-all-start.4 = ((f32[8,8,16,128]{3,2,1,0:T(8,128)}), f32[8,8,16,128]{3,2,1,0:T(8,128)}, u32[]{:S(2)}, u32[]{:S(2)}) async-start(f32[8,8,16,128]{3,2,1,0:T(8,128)} %bitcast.324), calls=%async_computation.4 | async-start | bytes 1048576 | tf_op jit(solution)/shard_map/all_to_all | solution.py:73
  300.7 5.1 copy-start.3
  313.5 5.1 copy-start.3
  323.2 13.9 %all-to-all-start.5 = ((f32[8,8,2048]{2,1,0:T(8,128)}), f32[8,8,2048]{2,1,0:T(8,128)S(1)}, u32[]{:S(2)}, u32[]{:S(2)}) async-start(f32[8,8,2048]{2,1,0:T(8,128)} %reshape.261), calls=%async_computation.5 | async-start | bytes 1048576 | tf_op jit(solution)/shard_map/all_to_all | solution.py:82
  326.9 43.2 %all-reduce.9.cloned.1.call-start = ((), (), s32[]{:S(2)}) async-start(), calls=%async_computation.9 | async-start | bytes 524288 | tf_op jit(solution)/shard_map/psum | solution.py:91
  417.0 14.4 %all-to-all-start.6 = ((f32[8,8,16,128]{3,2,1,0:T(8,128)}), f32[8,8,16,128]{3,2,1,0:T(8,128)}, u32[]{:S(2)}, u32[]{:S(2)}) async-start(f32[8,8,16,128]{3,2,1,0:T(8,128)} %bitcast.323), calls=%async_computation.6 | async-start | bytes 1048576 | tf_op jit(solution)/shard_map/all_to_all | solution.py:73
  438.0 5.1 copy-start.1
  450.8 5.1 copy-start.1
  460.6 13.9 %all-to-all-start.7 = ((f32[8,8,2048]{2,1,0:T(8,128)}), f32[8,8,2048]{2,1,0:T(8,128)S(1)}, u32[]{:S(2)}, u32[]{:S(2)}) async-start(f32[8,8,2048]{2,1,0:T(8,128)} %reshape.268), calls=%async_computation.7 | async-start | bytes 1048576 | tf_op jit(solution)/shard_map/all_to_all | solution.py:82
  464.2 42.2 %all-reduce.11.cloned.1.call-start = ((), (), s32[]{:S(2)}) async-start(), calls=%async_computation.10 | async-start | bytes 524288 | tf_op jit(solution)/shard_map/psum | solution.py:91
Sparse Core Ops, SparseCore 0:
  202.1 31.3 all-reduce.6
  339.6 30.4 all-reduce.8
  475.9 30.4 all-reduce.10
where the time goes:
time: 561 us; the launch traced here: 560 us
  waiting for transfers between devices  231 us (41%)
  blocking collectives  133 us (24%)
  matrix products  80.9 us (14%)
  local copies, waits for them, and re-layouts  43.4 us (8%)
  starting transfers between devices  34.9 us (6%)
  other arithmetic  21.7 us (4%)
  between operations  14.1 us (3%)
    psum x4, blocking collectives, gram_sums(): return lax.psum(values, 'wide')  133 us
    psum x3, waiting for transfers between devices, per_device(): summed_blocks = lax.psum(summed_blocks, 'narrow')  91.8 us
    all_to_all x1, waiting for transfers between devices, per_device(): lax.all_to_all(unit[local_ids], 'wide', split_axis=0, concat_axis=0, tile...  87.2 us
    all_to_all x3, waiting for transfers between devices, per_device(): lax.all_to_all(to_second.reshape(wide_count, capacity, vec_rows * BS), 'w...  29.2 us
    dot_general x6, matrix products, tile_terms(): jnp.einsum('pab,prb->pra', kernel_values, second_vec, precision=HIGH)  28.5 us
    all_to_all x3, waiting for transfers between devices, per_device(): lax.all_to_all(rows[local_ids], 'wide', split_axis=0, concat_axis=0, tile...  23.1 us
    dot_general x6, matrix products, tile_terms(): jnp.einsum('paf,pbf->pab', first_pts, second_pts, preferred_element_type=...  17.6 us
    dot_general x6, matrix products, tile_terms(): jnp.einsum('pab,pra->prb', kernel_values, first_vec, precision=HIGH)  16.5 us
  transfers between devices with their start and end apart: 11, of which 10 were waited for; matrix products, arithmetic and copies ran while one was open for 4% of the time, Pallas kernels for 0%

commit v1 on v0

--- a/solution.py
+++ b/solution.py
@@ -9,6 +9,18 @@
 EPSILON = 1e-06
 HIGH = lax.Precision.HIGHEST
 pair_group = 32
+
+
+def cut_along(x, dim, size):
+    lengths = x.shape
+    blocks = x.reshape(*lengths[:dim], size, lengths[dim] // size, *lengths[dim + 1 :])
+    return jnp.moveaxis(blocks, dim, 0)
+
+
+def joined_along(blocks, dim):
+    blocks = jnp.moveaxis(blocks, 0, dim)
+    shape = blocks.shape
+    return blocks.reshape(*shape[:dim], shape[dim] * shape[dim + 1], *shape[dim + 2 :])
 
 
 def unit_rows(points):
@@ -79,13 +91,15 @@
             (grouped(first_local), grouped(second_pts), grouped(first_vec), grouped(second_vec)),
         )
         to_first = to_first.reshape(pair_count, vec_rows * BS)
-        returned = lax.all_to_all(
-            to_second.reshape(wide_count, capacity, vec_rows * BS),
-            "wide",
-            split_axis=0,
-            concat_axis=0,
-            tiled=True,
-        )
+        array = to_second.reshape(wide_count, capacity, vec_rows * BS)
+        length, here = (lax.axis_size("wide"), lax.axis_index("wide"))
+        pieces = cut_along(array, 0, length)
+        outs = [pieces[here]]
+        for step_2 in range(1, length):
+            sent = pieces[here ^ step_2]
+            outs.append(lax.ppermute(sent, "wide", [(i, i ^ step_2) for i in range(length)]))
+        pieces = jnp.stack(outs)[here ^ jnp.arange(length)]
+        returned = joined_along(pieces, 0)
         terms = jnp.concatenate([to_first, returned.reshape(pair_count, vec_rows * BS)], axis=0)
         summed_blocks = jnp.dot(owners, terms, precision=HIGH)
         summed_blocks = lax.psum(summed_blocks, "narrow")

time: 561 us -> 574 us (1.023)
  starting transfers between devices: 34.9 us -> 57.7 us
  waiting for transfers between devices: 231 us -> 209 us
  local copies, waits for them, and re-layouts: 43.4 us -> 55.1 us
    ppermute x0 -> x21, starting transfers between devices: none -> 33.7 us  [per_device(): lax.ppermute(sent, 'wide', [(i, i ^ step_2) for i in range(length)])]
    all_to_all x3 -> x0, waiting for transfers between devices: 29.2 us -> none  [per_device(): lax.all_to_all(to_second.reshape(wide_count, capacity, vec_rows * BS), 'w...]
    all_to_all x3 -> x0, starting transfers between devices: 10.8 us -> none  [per_device(): lax.all_to_all(to_second.reshape(wide_count, capacity, vec_rows * BS), 'w...]
    ppermute x0 -> x21, waiting for transfers between devices: none -> 7.27 us  [per_device(): lax.ppermute(sent, 'wide', [(i, i ^ step_2) for i in range(length)])]
    unnamed x10 -> x28, local copies, waits for them, and re-layouts: 5.43 us -> 11.4 us
    reshape x3 -> x0, local copies, waits for them, and re-layouts: 5.75 us -> none  [per_device(): to_second.reshape(wide_count, capacity, vec_rows * BS)]
  transfers between devices with their start and end apart: 11 -> 29, of which waited for: 10 -> 11; matrix products, arithmetic and copies ran while one was open for 4% -> 5% of each run, Pallas kernels for 0% -> 0%
where the time goes in v1:
time: 574 us; the launch traced here: 573 us
  waiting for transfers between devices  209 us (36%)
  blocking collectives  133 us (23%)
  matrix products  81.1 us (14%)
  starting transfers between devices  57.7 us (10%)
  local copies, waits for them, and re-layouts  55.1 us (10%)
  other arithmetic  21.9 us (4%)
  between operations  14.3 us (2%)
    psum x4, blocking collectives, gram_sums(): return lax.psum(values, 'wide')  133 us
    psum x3, waiting for transfers between devices, per_device(): summed_blocks = lax.psum(summed_blocks, 'narrow')  91.8 us
    all_to_all x1, waiting for transfers between devices, per_device(): lax.all_to_all(unit[local_ids], 'wide', split_axis=0, concat_axis=0, tile...  87.1 us
    ppermute x21, starting transfers between devices, per_device(): lax.ppermute(sent, 'wide', [(i, i ^ step_2) for i in range(length)])  33.7 us
    dot_general x6, matrix products, tile_terms(): jnp.einsum('pab,prb->pra', kernel_values, second_vec, precision=HIGH)  28.5 us
    all_to_all x3, waiting for transfers between devices, per_device(): lax.all_to_all(rows[local_ids], 'wide', split_axis=0, concat_axis=0, tile...  23 us
    dot_general x6, matrix products, tile_terms(): jnp.einsum('paf,pbf->pab', first_pts, second_pts, preferred_element_type=...  17.6 us
    dot_general x6, matrix products, tile_terms(): jnp.einsum('pab,pra->prb', kernel_values, first_vec, precision=HIGH)  16.5 us
  transfers between devices with their start and end apart: 29, of which 11 were waited for; matrix products, arithmetic and copies ran while one was open for 5% of the time, Pallas kernels for 0%

profile of v1, /device:TPU:0, one launch (start us, length us, event | category | flops | bytes accessed | tf_op | source)
XLA Modules:
  0.0 572.7 jit_solution(17660439252031359821)
XLA Ops:
  8.7 7.3 %all-to-all-start = ((s32[8,1,8]{2,1,0:T(1,128)}), s32[8,1,8]{2,1,0:T(1,128)S(1)}, u32[]{:S(2)}, u32[]{:S(2)}) async-start(s32[8,1,8]{2,1,0:T(1,128)} %bitcast.22), calls=%async_computation | async-start | bytes 8192 | tf_op jit(solution)/shard_map/all_to_all | solution.py:55
  16.4 22.1 %psum.91 = f32[16,16]{1,0:T(8,128)S(1)} all-reduce(f32[16,16]{1,0:T(8,128)S(1)} %fusion.188), channel_id=1, replica_groups=mesh['wide'=8,'narrow'=4] {'wide'}, use_global_device_ids=true, to_apply=%region_1.0 | all-reduce | flops 256 | bytes 2048 | tf_op jit(solution)/shard_map/psum | solution.py:74
  43.2 2.2 fusion.78
  46.9 3.5 all-to-all-start.1
  50.4 1.9 fusion.79
  52.4 2.8 gather_fusion.4
  55.2 5.6 all-to-all-done.1
  60.8 4.5 all-to-all-start.2
  67.1 87.1 %all-to-all-done.2 = bf16[8,8,128,256]{3,2,1,0:T(8,128)(2,1)} async-done(((bf16[8,8,128,256]{3,2,1,0:T(8,128)(2,1)}), bf16[8,8,128,256]{3,2,1,0:T(8,128)(2,1)}, u32[]{:S(2)}, u32[]{:S(2)}) %all-to-all-start.2) | async-done | bytes 4194336 | tf_op jit(solution)/shard_map/all_to_all | solution.py:58
  155.9 23.6 %while.42 = (s32[]{:T(128)}, f32[2,32,16,128]{3,2,1,0:T(8,128)}, f32[2,32,16,128]{3,2,1,0:T(8,128)}, f32[2,32,16,128]{3,2,1,0:T(8,128)S(1)}, s32[2,32]{1,0:T(2,1...) while((s32[]{:T(128)}, f32[2,32,16,128]{3,2,1,0:T(8,128)}, ...), condition=%wide.region_5.8_spmd, body=%wide.region_4.7_spmd.sunk | while | flops 471860320 | bytes 17833084 | solution.py:89
  155.9 2.0 gather_fusion
  157.9 2.9 fusion.265
  160.8 4.1 fusion.266
  164.9 2.7 fusion.267
  167.6 2.0 gather_fusion
  169.6 2.9 fusion.265
  172.6 4.1 fusion.266
  176.7 2.8 fusion.267
  182.6 2.2 collective-permute-start.2
  184.8 3.7 collective-permute-start.4
  189.7 1.5 collective-permute-start.5
  191.9 2.5 collective-permute-start.6
  199.4 2.4 gather_fusion.6
  204.6 31.2 %all-reduce.7.cloned.1.call-done = f32[16,4096]{1,0:T(8,128)} async-done(((f32[16,4096]{1,0:T(8,128)}), f32[16,4096]{1,0:T(8,128)}) %all-reduce.7.cloned.1.call-update) | async-done | bytes 262160 | tf_op jit(solution)/shard_map/psum | solution.py:105
  237.9 37.1 %all-reduce.2 = (f32[16,16]{1,0:T(8,128)S(1)}, f32[16,16]{1,0:T(8,128)S(1)}, f32[16,16]{1,0:T(8,128)S(1)}) all-reduce(f32[16,16]{1,0:T(8,128)S(1)} %fusion.190, f32[16,16]{1,0:T(8,128)S(1)} %fusion.189, f32[16,16]{1,0:T(8,128)S(1)} %fusion.191), channel_id=1, replica_groups=mesh['wide'=8,'narrow'=4] {'wide'}, use_global_device_ids=true, to_apply=%region_8.11 | all-reduce | flops 768 | bytes 6144 | tf_op jit(solution)/shard_map/psum | solution.py:74
  282.1 4.1 all-to-all-start.3
  287.7 8.8 %all-to-all-done.3 = f32[8,8,16,128]{3,2,1,0:T(8,128)} async-done(((f32[8,8,16,128]{3,2,1,0:T(8,128)}), f32[8,8,16,128]{3,2,1,0:T(8,128)}, u32[]{:S(2)}, u32[]{:S(2)}) %all-to-all-start.3) | async-done | bytes 524320 | tf_op jit(solution)/shard_map/all_to_all | solution.py:85
  298.2 25.6 %while.43 = (s32[]{:T(128)}, f32[2,32,16,128]{3,2,1,0:T(8,128)}, f32[2,32,16,128]{3,2,1,0:T(8,128)}, f32[2,32,16,128]{3,2,1,0:T(8,128)}, s32[2,32]{1,0:T(2,128)S...) while((s32[]{:T(128)}, f32[2,32,16,128]{3,2,1,0:T(8,128)}, ...), condition=%wide.region_11.14_spmd, body=%wide.region_10.13_spmd.sunk | while | flops 471860320 | bytes 17833084 | solution.py:89
  298.2 2.0 gather_fusion.1
  300.2 2.9 fusion.273
  303.2 5.1 fusion.274
  308.2 2.7 fusion.275
  311.0 2.0 gather_fusion.1
  313.0 2.9 fusion.273
  315.9 5.1 fusion.274
  321.0 2.8 fusion.275
  327.2 1.8 collective-permute-start.9
  329.9 3.1 collective-permute-start.11
  334.1 1.5 collective-permute-start.12
  336.3 2.3 collective-permute-start.13
  343.9 2.4 gather_fusion.9
  349.1 30.1 %all-reduce.9.cloned.1.call-done = f32[16,4096]{1,0:T(8,128)} async-done(((f32[16,4096]{1,0:T(8,128)}), f32[16,4096]{1,0:T(8,128)}) %all-reduce.9.cloned.1.call-update) | async-done | bytes 262160 | tf_op jit(solution)/shard_map/psum | solution.py:105
  379.2 2.0 convolution_subtract_fusion.3
  382.1 37.1 %all-reduce.1 = (f32[16,16]{1,0:T(8,128)S(1)}, f32[16,16]{1,0:T(8,128)S(1)}, f32[16,16]{1,0:T(8,128)S(1)}) all-reduce(f32[16,16]{1,0:T(8,128)S(1)} %fusion.193, f32[16,16]{1,0:T(8,128)S(1)} %fusion.192, f32[16,16]{1,0:T(8,128)S(1)} %fusion.194), channel_id=1, replica_groups=mesh['wide'=8,'narrow'=4] {'wide'}, use_global_device_ids=true, to_apply=%region_14.17 | all-reduce | flops 768 | bytes 6144 | tf_op jit(solution)/shard_map/psum | solution.py:74
  426.3 4.1 all-to-all-start.4
  432.2 8.5 %all-to-all-done.4 = f32[8,8,16,128]{3,2,1,0:T(8,128)} async-done(((f32[8,8,16,128]{3,2,1,0:T(8,128)}), f32[8,8,16,128]{3,2,1,0:T(8,128)}, u32[]{:S(2)}, u32[]{:S(2)}) %all-to-all-start.4) | async-done | bytes 524320 | tf_op jit(solution)/shard_map/all_to_all | solution.py:85
  442.4 25.6 %while.44 = (s32[]{:T(128)}, f32[2,32,16,128]{3,2,1,0:T(8,128)}, f32[2,32,16,128]{3,2,1,0:T(8,128)}, f32[2,32,16,128]{3,2,1,0:T(8,128)}, s32[2,32]{1,0:T(2,128)S...) while((s32[]{:T(128)}, f32[2,32,16,128]{3,2,1,0:T(8,128)}, ...), condition=%wide.region_17.20_spmd, body=%wide.region_16.19_spmd.sunk | while | flops 471860320 | bytes 17833084 | solution.py:89
  442.4 2.0 gather_fusion.2
  444.4 2.9 fusion.281
  447.3 5.1 fusion.282
  452.4 2.7 fusion.283
  455.2 2.0 gather_fusion.2
  457.2 2.9 fusion.281
  460.1 5.1 fusion.282
  465.2 2.8 fusion.283
  471.4 1.8 collective-permute-start.16
  474.0 3.0 collective-permute-start.18
  478.2 1.5 collective-permute-start.19
  479.8 2.4 collective-permute-start.20
  482.3 2.1 collective-permute-done.19
  484.4 2.5 collective-permute-done.20
  488.7 30.5 %all-reduce.11.cloned.1.call-done = f32[16,4096]{1,0:T(8,128)} async-done(((f32[16,4096]{1,0:T(8,128)}), f32[16,4096]{1,0:T(8,128)}) %all-reduce.11.cloned.1.call-update) | async-done | bytes 262160 | tf_op jit(solution)/shard_map/psum | solution.py:105
  519.3 2.0 convolution_subtract_fusion.1
  522.2 37.1 %all-reduce = (f32[16,16]{1,0:T(8,128)S(1)}, f32[16,16]{1,0:T(8,128)S(1)}, f32[16,16]{1,0:T(8,128)S(1)}) all-reduce(f32[16,16]{1,0:T(8,128)S(1)} %fusion.196, f32[16,16]{1,0:T(8,128)S(1)} %fusion.195, f32[16,16]{1,0:T(8,128)S(1)} %fusion.197), channel_id=1, replica_groups=mesh['wide'=8,'narrow'=4] {'wide'}, use_global_device_ids=true, to_apply=%region_20.23 | all-reduce | flops 768 | bytes 6144 | tf_op jit(solution)/shard_map/psum | solution.py:74
  (197 shorter events, 77.1 us)
Async XLA Ops:
  7.2 8.8 %copy-start = (f32[16,4096]{1,0:T(8,128)S(1)}, f32[16,4096]{1,0:T(8,128)}, u32[]{:S(2)}) copy-start(f32[16,4096]{1,0:T(8,128)} %param.13) | copy-start | bytes 786436
  7.2 38.2 %copy-start.4 = (s32[2,64]{1,0:T(2,128)S(1)}, s32[2,64]{1,0:T(2,128)}, u32[]{:S(2)}) copy-start(s32[2,64]{1,0:T(2,128)} %param.14) | copy-start | bytes 1540
  8.7 36.7 %all-to-all-start = ((s32[8,1,8]{2,1,0:T(1,128)}), s32[8,1,8]{2,1,0:T(1,128)S(1)}, u32[]{:S(2)}, u32[]{:S(2)}) async-start(s32[8,1,8]{2,1,0:T(1,128)} %bitcast.22), calls=%async_computation | async-start | bytes 8192 | tf_op jit(solution)/shard_map/all_to_all | solution.py:55
  46.9 13.9 %all-to-all-start.1 = ((f32[8,8,16,128]{3,2,1,0:T(8,128)}), f32[8,8,16,128]{3,2,1,0:T(8,128)S(1)}, u32[]{:S(2)}, u32[]{:S(2)}) async-start(f32[8,8,16,128]{3,2,1,0:T(8,128)} %bitcast.29), calls=%async_computation.1 | async-start | bytes 1048576 | tf_op jit(solution)/shard_map/all_to_all | solution.py:85
  60.8 93.4 %all-to-all-start.2 = ((bf16[8,8,128,256]{3,2,1,0:T(8,128)(2,1)}), bf16[8,8,128,256]{3,2,1,0:T(8,128)(2,1)}, u32[]{:S(2)}, u32[]{:S(2)}) async-start(bf16[8,8,128,256]{3,2,1,0:T(8,128)(2,1)} %bitcast.401), calls=%async_computation.2 | async-start | bytes 8388608 | tf_op jit(solution)/shard_map/all_to_all | solution.py:58
  65.4 170.5 %all-reduce.7.cloned.1.call-start = ((), (), s32[]{:S(2)}) async-start(), calls=%async_computation.5 | async-start | bytes 524288 | tf_op jit(solution)/shard_map/psum | solution.py:105
  160.8 4.1 copy-start.2
  172.6 4.1 copy-start.2
  181.3 8.4 %collective-permute-start = (f32[1,8,2048]{2,1,0:T(8,128)S(1)}, f32[1,8,2048]{2,1,0:T(8,128)S(1)}, u32[]{:S(2)}, u32[]{:S(2)}) collective-permute-start(f32[1,8,2048]{2,1,0:T(8,128)S(1)} %get-tuple-element.399), channel_id=1, source_target_pairs={{0,4},{4,0},{8,12},{12,8},{16,20},{20,16},{24,28},{28,24},{1,5},{5... | collective-permute-start | bytes 196616 | tf_op jit(solution)/shard_map/ppermute | solution.py:100
  182.6 9.2 %collective-permute-start.1 = (f32[1,8,2048]{2,1,0:T(8,128)S(1)}, f32[1,8,2048]{2,1,0:T(8,128)S(1)}, u32[]{:S(2)}, u32[]{:S(2)}) collective-permute-start(f32[1,8,2048]{2,1,0:T(8,128)S(1)} %get-tuple-element.398), channel_id=1, source_target_pairs={{0,8},{4,12},{8,0},{12,4},{16,24},{20,28},{24,16},{28,20},{1,9},{5... | collective-permute-start | bytes 196616 | tf_op jit(solution)/shard_map/ppermute | solution.py:100
  182.6 12.4 %collective-permute-start.2 = (f32[1,8,2048]{2,1,0:T(8,128)S(1)}, f32[1,8,2048]{2,1,0:T(8,128)S(1)}, u32[]{:S(2)}, u32[]{:S(2)}) collective-permute-start(f32[1,8,2048]{2,1,0:T(8,128)S(1)} %get-tuple-element.397), channel_id=1, source_target_pairs={{0,12},{4,8},{8,4},{12,0},{16,28},{20,24},{24,20},{28,16},{1,13},{... | collective-permute-start | bytes 196616 | tf_op jit(solution)/shard_map/ppermute | solution.py:100
  184.8 10.8 %collective-permute-start.3 = (f32[1,8,2048]{2,1,0:T(8,128)S(1)}, f32[1,8,2048]{2,1,0:T(8,128)S(1)}, u32[]{:S(2)}, u32[]{:S(2)}) collective-permute-start(f32[1,8,2048]{2,1,0:T(8,128)S(1)} %get-tuple-element.396), channel_id=1, source_target_pairs={{0,16},{4,20},{8,24},{12,28},{16,0},{20,4},{24,8},{28,12},{1,17},{... | collective-permute-start | bytes 196616 | tf_op jit(solution)/shard_map/ppermute | solution.py:100
  184.8 11.5 %collective-permute-start.4 = (f32[1,8,2048]{2,1,0:T(8,128)S(1)}, f32[1,8,2048]{2,1,0:T(8,128)S(1)}, u32[]{:S(2)}, u32[]{:S(2)}) collective-permute-start(f32[1,8,2048]{2,1,0:T(8,128)S(1)} %get-tuple-element.395), channel_id=1, source_target_pairs={{0,20},{4,16},{8,28},{12,24},{16,4},{20,0},{24,12},{28,8},{1,21},{... | collective-permute-start | bytes 196616 | tf_op jit(solution)/shard_map/ppermute | solution.py:100
  189.7 7.2 %collective-permute-start.5 = (f32[1,8,2048]{2,1,0:T(8,128)S(1)}, f32[1,8,2048]{2,1,0:T(8,128)S(1)}, u32[]{:S(2)}, u32[]{:S(2)}) collective-permute-start(f32[1,8,2048]{2,1,0:T(8,128)S(1)} %get-tuple-element.394), channel_id=1, source_target_pairs={{0,24},{4,28},{8,16},{12,20},{16,8},{20,12},{24,0},{28,4},{1,25},{... | collective-permute-start | bytes 196616 | tf_op jit(solution)/shard_map/ppermute | solution.py:100
  191.9 7.0 %collective-permute-start.6 = (f32[1,8,2048]{2,1,0:T(8,128)S(1)}, f32[1,8,2048]{2,1,0:T(8,128)S(1)}, u32[]{:S(2)}, u32[]{:S(2)}) collective-permute-start(f32[1,8,2048]{2,1,0:T(8,128)S(1)} %get-tuple-element.393), channel_id=1, source_target_pairs={{0,28},{4,24},{8,20},{12,16},{16,12},{20,8},{24,4},{28,0},{1,29},{... | collective-permute-start | bytes 196616 | tf_op jit(solution)/shard_map/ppermute | solution.py:100
  282.1 14.4 %all-to-all-start.3 = ((f32[8,8,16,128]{3,2,1,0:T(8,128)}), f32[8,8,16,128]{3,2,1,0:T(8,128)}, u32[]{:S(2)}, u32[]{:S(2)}) async-start(f32[8,8,16,128]{3,2,1,0:T(8,128)} %bitcast.413), calls=%async_computation.3 | async-start | bytes 1048576 | tf_op jit(solution)/shard_map/all_to_all | solution.py:85
  286.3 93.0 %all-reduce.9.cloned.1.call-start = ((), (), s32[]{:S(2)}) async-start(), calls=%async_computation.6 | async-start | bytes 524288 | tf_op jit(solution)/shard_map/psum | solution.py:105
  303.2 5.1 copy-start.3
  315.9 5.1 copy-start.3
  325.6 8.5 %collective-permute-start.7 = (f32[1,8,2048]{2,1,0:T(8,128)S(1)}, f32[1,8,2048]{2,1,0:T(8,128)S(1)}, u32[]{:S(2)}, u32[]{:S(2)}) collective-permute-start(f32[1,8,2048]{2,1,0:T(8,128)S(1)} %get-tuple-element.391), channel_id=1, source_target_pairs={{0,4},{4,0},{8,12},{12,8},{16,20},{20,16},{24,28},{28,24},{1,5},{5... | collective-permute-start | bytes 196616 | tf_op jit(solution)/shard_map/ppermute | solution.py:100
  327.1 9.2 %collective-permute-start.8 = (f32[1,8,2048]{2,1,0:T(8,128)S(1)}, f32[1,8,2048]{2,1,0:T(8,128)S(1)}, u32[]{:S(2)}, u32[]{:S(2)}) collective-permute-start(f32[1,8,2048]{2,1,0:T(8,128)S(1)} %get-tuple-element.390), channel_id=1, source_target_pairs={{0,8},{4,12},{8,0},{12,4},{16,24},{20,28},{24,16},{28,20},{1,9},{5... | collective-permute-start | bytes 196616 | tf_op jit(solution)/shard_map/ppermute | solution.py:100
  327.2 12.0 %collective-permute-start.9 = (f32[1,8,2048]{2,1,0:T(8,128)S(1)}, f32[1,8,2048]{2,1,0:T(8,128)S(1)}, u32[]{:S(2)}, u32[]{:S(2)}) collective-permute-start(f32[1,8,2048]{2,1,0:T(8,128)S(1)} %get-tuple-element.389), channel_id=1, source_target_pairs={{0,12},{4,8},{8,4},{12,0},{16,28},{20,24},{24,20},{28,16},{1,13},{... | collective-permute-start | bytes 196616 | tf_op jit(solution)/shard_map/ppermute | solution.py:100
  329.1 10.8 %collective-permute-start.10 = (f32[1,8,2048]{2,1,0:T(8,128)S(1)}, f32[1,8,2048]{2,1,0:T(8,128)S(1)}, u32[]{:S(2)}, u32[]{:S(2)}) collective-permute-start(f32[1,8,2048]{2,1,0:T(8,128)S(1)} %get-tuple-element.388), channel_id=1, source_target_pairs={{0,16},{4,20},{8,24},{12,28},{16,0},{20,4},{24,8},{28,12},{1,17},{... | collective-permute-start | bytes 196616 | tf_op jit(solution)/shard_map/ppermute | solution.py:100
  329.9 10.7 %collective-permute-start.11 = (f32[1,8,2048]{2,1,0:T(8,128)S(1)}, f32[1,8,2048]{2,1,0:T(8,128)S(1)}, u32[]{:S(2)}, u32[]{:S(2)}) collective-permute-start(f32[1,8,2048]{2,1,0:T(8,128)S(1)} %get-tuple-element.387), channel_id=1, source_target_pairs={{0,20},{4,16},{8,28},{12,24},{16,4},{20,0},{24,12},{28,8},{1,21},{... | collective-permute-start | bytes 196616 | tf_op jit(solution)/shard_map/ppermute | solution.py:100
  334.1 7.1 %collective-permute-start.12 = (f32[1,8,2048]{2,1,0:T(8,128)S(1)}, f32[1,8,2048]{2,1,0:T(8,128)S(1)}, u32[]{:S(2)}, u32[]{:S(2)}) collective-permute-start(f32[1,8,2048]{2,1,0:T(8,128)S(1)} %get-tuple-element.386), channel_id=1, source_target_pairs={{0,24},{4,28},{8,16},{12,20},{16,8},{20,12},{24,0},{28,4},{1,25},{... | collective-permute-start | bytes 196616 | tf_op jit(solution)/shard_map/ppermute | solution.py:100
  336.3 7.0 %collective-permute-start.13 = (f32[1,8,2048]{2,1,0:T(8,128)S(1)}, f32[1,8,2048]{2,1,0:T(8,128)S(1)}, u32[]{:S(2)}, u32[]{:S(2)}) collective-permute-start(f32[1,8,2048]{2,1,0:T(8,128)S(1)} %get-tuple-element.385), channel_id=1, source_target_pairs={{0,28},{4,24},{8,20},{12,16},{16,12},{20,8},{24,4},{28,0},{1,29},{... | collective-permute-start | bytes 196616 | tf_op jit(solution)/shard_map/ppermute | solution.py:100
  426.3 14.4 %all-to-all-start.4 = ((f32[8,8,16,128]{3,2,1,0:T(8,128)}), f32[8,8,16,128]{3,2,1,0:T(8,128)}, u32[]{:S(2)}, u32[]{:S(2)}) async-start(f32[8,8,16,128]{3,2,1,0:T(8,128)} %bitcast.412), calls=%async_computation.4 | async-start | bytes 1048576 | tf_op jit(solution)/shard_map/all_to_all | solution.py:85
  430.4 88.8 %all-reduce.11.cloned.1.call-start = ((), (), s32[]{:S(2)}) async-start(), calls=%async_computation.7 | async-start | bytes 524288 | tf_op jit(solution)/shard_map/psum | solution.py:105
  447.3 5.1 copy-start.1
  460.1 5.1 copy-start.1
  469.2 9.1 %collective-permute-start.14 = (f32[1,8,2048]{2,1,0:T(8,128)S(1)}, f32[1,8,2048]{2,1,0:T(8,128)S(1)}, u32[]{:S(2)}, u32[]{:S(2)}) collective-permute-start(f32[1,8,2048]{2,1,0:T(8,128)S(1)} %get-tuple-element.383), channel_id=1, source_target_pairs={{0,4},{4,0},{8,12},{12,8},{16,20},{20,16},{24,28},{28,24},{1,5},{5... | collective-permute-start | bytes 196616 | tf_op jit(solution)/shard_map/ppermute | solution.py:100
  471.2 8.6 %collective-permute-start.15 = (f32[1,8,2048]{2,1,0:T(8,128)S(1)}, f32[1,8,2048]{2,1,0:T(8,128)S(1)}, u32[]{:S(2)}, u32[]{:S(2)}) collective-permute-start(f32[1,8,2048]{2,1,0:T(8,128)S(1)} %get-tuple-element.382), channel_id=1, source_target_pairs={{0,8},{4,12},{8,0},{12,4},{16,24},{20,28},{24,16},{28,20},{1,9},{5... | collective-permute-start | bytes 196616 | tf_op jit(solution)/shard_map/ppermute | solution.py:100
  471.4 10.9 %collective-permute-start.16 = (f32[1,8,2048]{2,1,0:T(8,128)S(1)}, f32[1,8,2048]{2,1,0:T(8,128)S(1)}, u32[]{:S(2)}, u32[]{:S(2)}) collective-permute-start(f32[1,8,2048]{2,1,0:T(8,128)S(1)} %get-tuple-element.381), channel_id=1, source_target_pairs={{0,12},{4,8},{8,4},{12,0},{16,28},{20,24},{24,20},{28,16},{1,13},{... | collective-permute-start | bytes 196616 | tf_op jit(solution)/shard_map/ppermute | solution.py:100
  473.2 9.0 %collective-permute-start.17 = (f32[1,8,2048]{2,1,0:T(8,128)S(1)}, f32[1,8,2048]{2,1,0:T(8,128)S(1)}, u32[]{:S(2)}, u32[]{:S(2)}) collective-permute-start(f32[1,8,2048]{2,1,0:T(8,128)S(1)} %get-tuple-element.380), channel_id=1, source_target_pairs={{0,16},{4,20},{8,24},{12,28},{16,0},{20,4},{24,8},{28,12},{1,17},{... | collective-permute-start | bytes 196616 | tf_op jit(solution)/shard_map/ppermute | solution.py:100
  474.0 8.3 %collective-permute-start.18 = (f32[1,8,2048]{2,1,0:T(8,128)S(1)}, f32[1,8,2048]{2,1,0:T(8,128)S(1)}, u32[]{:S(2)}, u32[]{:S(2)}) collective-permute-start(f32[1,8,2048]{2,1,0:T(8,128)S(1)} %get-tuple-element.379), channel_id=1, source_target_pairs={{0,20},{4,16},{8,28},{12,24},{16,4},{20,0},{24,12},{28,8},{1,21},{... | collective-permute-start | bytes 196616 | tf_op jit(solution)/shard_map/ppermute | solution.py:100
  478.2 6.1 %collective-permute-start.19 = (f32[1,8,2048]{2,1,0:T(8,128)S(1)}, f32[1,8,2048]{2,1,0:T(8,128)S(1)}, u32[]{:S(2)}, u32[]{:S(2)}) collective-permute-start(f32[1,8,2048]{2,1,0:T(8,128)S(1)} %get-tuple-element.378), channel_id=1, source_target_pairs={{0,24},{4,28},{8,16},{12,20},{16,8},{20,12},{24,0},{28,4},{1,25},{... | collective-permute-start | bytes 196616 | tf_op jit(solution)/shard_map/ppermute | solution.py:100
  479.8 7.0 %collective-permute-start.20 = (f32[1,8,2048]{2,1,0:T(8,128)S(1)}, f32[1,8,2048]{2,1,0:T(8,128)S(1)}, u32[]{:S(2)}, u32[]{:S(2)}) collective-permute-start(f32[1,8,2048]{2,1,0:T(8,128)S(1)} %get-tuple-element.377), channel_id=1, source_target_pairs={{0,28},{4,24},{8,20},{12,16},{16,12},{20,8},{24,4},{28,0},{1,29},{... | collective-permute-start | bytes 196616 | tf_op jit(solution)/shard_map/ppermute | solution.py:100
Sparse Core Ops, SparseCore 0:
  204.3 31.4 all-reduce.6
  348.8 30.3 all-reduce.8
  488.8 30.3 all-reduce.10
